TPU v7x, 512 devices: a whole 4x8x8 slice. The times are simulated.
512 devices in a mesh: src: 16 (over z_hi, x, core), rows: 32 (over z_lo, y).
Axes of the slice: x: 4, y: 8, z: 8 (z_hi: 2, z_lo: 4; z = z_hi * 4 + z_lo), core: 2. Of those that a mesh axis runs over, the one named last changes fastest.
Arguments:
- mask_param: float32 [512, 8192], P('rows'), may hold values from -6 to 6
- target: int32 [512, 8192], P('rows', 'src'), may hold values 0 or 1
- source_weight: float32 [16], replicated, may hold values from 0.25 to 4
- row_shift: int32 [16], replicated, may hold values from -8 to 8
- col_shift: int32 [16], replicated, may hold values from -32 to 32
Outputs:
- mask_grad: float32 [512, 8192], P('rows', 'src')
All inputs are finite; a program needn't handle non-finite values. No bound on the sum of `target` on one device may be relied on, other than what follows from the above.
Results may differ from a plain program's by a relative error of at most 0.0003.
Values sent between devices are 32-bit elements; how exact they have to be, the bound alone decides.
No kernel may reach another device: no remote copies, remote signals or barrier semaphores. Data moves between devices by JAX's collectives and lax.ppermute only.
A program may use at most 64 MiB of HBM per device.

v0:
```python
import math
import jax
import jax.numpy as jnp
from jax import lax
from jax.sharding import PartitionSpec as P

steepness = 250.0
threshold_level = 0.25
loss_weight = 8.0
highest = lax.Precision.HIGHEST


def product(matrix_left, matrix_right):
    return jnp.dot(matrix_left, matrix_right, precision=highest, preferred_element_type=jnp.float32)


def product_nt(matrix_left, matrix_right):
    return lax.dot_general(
        matrix_left,
        matrix_right,
        (((1,), (1,)), ((), ())),
        precision=highest,
        preferred_element_type=jnp.float32,
    )


def product_tn(matrix_left, matrix_right):
    return lax.dot_general(
        matrix_left,
        matrix_right,
        (((0,), (0,)), ((), ())),
        precision=highest,
        preferred_element_type=jnp.float32,
    )


def centered(number):
    return jnp.arange(number, dtype=jnp.int32) - number // 2


def phases(frequency, position, period):
    angles = jnp.mod(position[:, None] * frequency[None, :], period).astype(jnp.float32) * (
        2.0 * math.pi / period
    )
    return (jnp.cos(angles), jnp.sin(angles))


def pupil_mask(row_offset, col_offset, band_rows, band_cols):
    radius_rows = band_rows // 4
    radius_cols = band_cols // 4
    row_term = (centered(band_rows) + row_offset) ** 2 * (radius_cols * radius_cols)
    col_term = (centered(band_cols) + col_offset) ** 2 * (radius_rows * radius_rows)
    limit_value = (radius_rows * radius_cols) ** 2
    return (row_term[:, None] + col_term[None, :] <= limit_value).astype(jnp.float32)


def columns_forward(real_part, imag_part, column_start, band_cols, total_columns):
    row_count, col_width = real_part.shape
    block_width = min(512, col_width)
    block_count = col_width // block_width
    frequency = centered(band_cols)
    base_cos, base_sin = phases(frequency, jnp.arange(block_width, dtype=jnp.int32), total_columns)
    starts = column_start + block_width * jnp.arange(block_count, dtype=jnp.int32)
    twist_cos, twist_sin = phases(frequency, starts, total_columns)
    stack_rows = row_count * block_count
    if imag_part is None:
        flat_real = real_part.reshape(stack_rows, block_width)
        part_real = product(flat_real, base_cos)
        part_imag = -product(flat_real, base_sin)
    else:
        stacked = jnp.concatenate(
            [
                real_part.reshape(stack_rows, block_width),
                imag_part.reshape(stack_rows, block_width),
            ],
            axis=0,
        )
        with_cos = product(stacked, base_cos)
        with_sin = product(stacked, base_sin)
        part_real = with_cos[:stack_rows] + with_sin[stack_rows:]
        part_imag = with_cos[stack_rows:] - with_sin[:stack_rows]
    part_real = part_real.reshape(row_count, block_count, band_cols)
    part_imag = part_imag.reshape(row_count, block_count, band_cols)
    out_real = jnp.sum(part_real * twist_cos + part_imag * twist_sin, axis=1)
    out_imag = jnp.sum(part_imag * twist_cos - part_real * twist_sin, axis=1)
    return (out_real, out_imag)


def rows_forward(real_part, imag_part, row_start, band_rows, total_rows):
    position = row_start + jnp.arange(real_part.shape[0], dtype=jnp.int32)
    row_cos, row_sin = phases(centered(band_rows), position, total_rows)
    out_real = product_tn(row_cos, real_part) + product_tn(row_sin, imag_part)
    out_imag = product_tn(row_cos, imag_part) - product_tn(row_sin, real_part)
    return (out_real, out_imag)


def rows_inverse(real_part, imag_part, row_start, row_count, total_rows):
    position = row_start + jnp.arange(row_count, dtype=jnp.int32)
    row_cos, row_sin = phases(centered(real_part.shape[0]), position, total_rows)
    out_real = product(row_cos, real_part) - product(row_sin, imag_part)
    out_imag = product(row_cos, imag_part) + product(row_sin, real_part)
    return (out_real, out_imag)


def columns_inverse(real_part, imag_part, column_start, width_out, total_columns):
    row_count, band_cols = real_part.shape
    block_width = min(512, width_out)
    block_count = width_out // block_width
    frequency = centered(band_cols)
    base_cos, base_sin = phases(frequency, jnp.arange(block_width, dtype=jnp.int32), total_columns)
    starts = column_start + block_width * jnp.arange(block_count, dtype=jnp.int32)
    twist_cos, twist_sin = phases(frequency, starts, total_columns)
    turned_real = real_part[:, None, :] * twist_cos - imag_part[:, None, :] * twist_sin
    turned_imag = real_part[:, None, :] * twist_sin + imag_part[:, None, :] * twist_cos
    stack_rows = row_count * block_count
    stacked = jnp.concatenate(
        [turned_real.reshape(stack_rows, band_cols), turned_imag.reshape(stack_rows, band_cols)],
        axis=0,
    )
    with_cos = product_nt(stacked, base_cos)
    with_sin = product_nt(stacked, base_sin)
    field_real = (with_cos[:stack_rows] - with_sin[stack_rows:]).reshape(row_count, width_out)
    field_imag = (with_sin[:stack_rows] + with_cos[stack_rows:]).reshape(row_count, width_out)
    return (field_real, field_imag)


def resist_slope(intensity, target):
    resist = jax.nn.sigmoid(steepness * (intensity - threshold_level))
    return (
        2.0
        * loss_weight
        * (resist - target.astype(jnp.float32))
        * steepness
        * resist
        * (1.0 - resist)
    )


def local(mask_param, target, source_weight, row_shift, col_shift):
    row_block, total_columns = mask_param.shape
    src_count = lax.axis_size("src")
    src_index = lax.axis_index("src")
    row_index = lax.axis_index("rows")
    total_rows = row_block * lax.axis_size("rows")
    band_rows = total_rows // 16
    band_cols = total_columns // 64
    col_share = total_columns // src_count
    local_points = source_weight.shape[0] // src_count
    row_start = row_index * row_block
    share_start = src_index * col_share
    unit_scale = 1.0 / math.sqrt(total_rows * total_columns)
    opening = jax.nn.sigmoid(mask_param)
    all_weights = source_weight / jnp.sum(source_weight)
    col_real, col_imag = columns_forward(opening, None, 0, band_cols, total_columns)
    part_real, part_imag = rows_forward(col_real, col_imag, row_start, band_rows, total_rows)
    band_real, band_imag = lax.psum((part_real * unit_scale, part_imag * unit_scale), "rows")
    my_weights = lax.dynamic_slice_in_dim(all_weights, src_index * local_points, local_points)
    my_rows = lax.dynamic_slice_in_dim(row_shift, src_index * local_points, local_points)
    my_cols = lax.dynamic_slice_in_dim(col_shift, src_index * local_points, local_points)
    source_point = 0
    opened = pupil_mask(my_rows[source_point], my_cols[source_point], band_rows, band_cols)
    head_real, head_imag = rows_inverse(
        band_real * opened * unit_scale,
        band_imag * opened * unit_scale,
        row_start,
        row_block,
        total_rows,
    )
    field_real, field_imag = columns_inverse(head_real, head_imag, 0, total_columns, total_columns)
    intensity_part = my_weights[source_point] * (field_real * field_real + field_imag * field_imag)
    field_list = [(field_real, field_imag)]
    pupil_list = [opened]
    intensity = lax.psum_scatter(intensity_part, "src", scatter_dimension=1, tiled=True)
    slope_share = resist_slope(intensity, target)
    slope = lax.all_gather(slope_share, "src", axis=1, tiled=True)
    source_point = 0
    field_real, field_imag = field_list[source_point]
    factor = 2.0 * my_weights[source_point] * slope
    cot_real, cot_imag = columns_forward(
        factor * field_real, factor * field_imag, 0, band_cols, total_columns
    )
    back_real, back_imag = rows_forward(cot_real, cot_imag, row_start, band_rows, total_rows)
    adjoint_real = pupil_list[source_point] * back_real
    adjoint_imag = pupil_list[source_point] * back_imag
    adjoint_real, adjoint_imag = lax.psum(
        (adjoint_real * unit_scale, adjoint_imag * unit_scale), ("src", "rows")
    )
    head_real, head_imag = rows_inverse(
        adjoint_real * unit_scale, adjoint_imag * unit_scale, row_start, row_block, total_rows
    )
    grad_real, grad_imag = columns_inverse(
        head_real, head_imag, share_start, col_share, total_columns
    )
    own_open = lax.dynamic_slice_in_dim(opening, share_start, col_share, 1)
    return grad_real * own_open * (1.0 - own_open)


def solution(mesh):
    placed = (P("rows", None), P("rows", "src"), P(), P(), P())
    return jax.shard_map(
        local, mesh=mesh, in_specs=placed, out_specs=P("rows", "src"), check_vma=False
    )
```

profile of v0, /device:TPU:1, one launch (start us, length us, event | category | flops | bytes accessed | tf_op | source)
XLA Modules:
  0.0 408.0 jit_solution(5263452524671067689)
XLA Ops:
  6.5 0.0 reduce-scatter.2.cloned.1.call-start
  6.5 1.2 add_divide_fusion
  7.7 0.1 reshape.193
  7.8 0.1 fusion.73
  8.0 1.5 convolution_negate_fusion
  9.5 0.3 copy.6
  9.9 1.6 add_reduce_fusion.1
  11.4 0.3 fusion.86
  11.8 0.3 fusion.83
  12.1 0.3 fusion.7
  12.4 0.3 fusion.6
  12.8 0.0 copy-start.1
  12.8 0.6 copy-done.1
  13.5 0.6 dynamic_slice.13
  14.0 0.0 copy-start.2
  14.0 0.7 multiply_multiply_fusion.2
  14.7 0.0 copy-done.2
  14.7 0.6 dynamic_slice.12
  15.3 0.7 multiply_multiply_fusion.3
  16.0 128.9 %all-reduce.1 = (f32[32,128]{1,0:T(8,128)S(1)}, f32[32,128]{1,0:T(8,128)S(1)}) all-reduce(f32[32,128]{1,0:T(8,128)S(1)} %fusion.6, f32[32,128]{1,0:T(8,128)S(1)} %fusion.7), channel_id=1, replica_groups=mesh['src'=16,'rows'=32] {'rows'}, use_global_device_ids=true, to_apply=%region_4.5 | all-reduce | flops 8192 | bytes 65536 | tf_op jit(solution)/shard_map/psum | solution.py:156
  144.9 0.2 fusion.37
  145.1 0.3 fusion.38
  145.4 0.3 convolution_subtract_fusion.4
  145.6 0.3 convolution_add_fusion.3
  145.9 1.9 fusion.16
  147.9 1.9 fusion.17
  149.8 0.2 slice_add_fusion
  150.0 0.1 reshape.195
  150.2 0.0 copy-start.3
  150.2 0.1 reshape.196
  150.3 0.5 copy-done.3
  150.8 0.6 reduce_sum.45
  151.4 0.6 broadcast_divide_fusion
  152.1 0.6 dynamic_slice.14
  152.7 1.5 add_multiply_fusion
  154.2 0.0 copy-start
  154.2 0.0 reduce-scatter.2.cloned.1.call-update
  154.8 0.1 fusion.123
  154.9 107.6 %reduce-scatter.2.cloned.1.call-done = f32[16,512]{1,0:T(8,128)} async-done(((f32[16,8192]{1,0:T(8,128)}), f32[16,512]{1,0:T(8,128)}) %reduce-scatter.2.cloned.1.call-update) | async-done | bytes 32784 | tf_op jit(solution)/shard_map/reduce_scatter | solution.py:173
  262.5 0.0 copy-done
  262.5 0.8 subtract_multiply_fusion
  263.3 30.5 %all_gather.3 = f32[16,8192]{1,0:T(8,128)S(1)} all-gather(f32[16,512]{1,0:T(8,128)S(1)} %subtract_multiply_fusion), channel_id=1, replica_groups=mesh['src'=16,'rows'=32] {'src'}, dimensions={1}, use_global_device_ids=true | all-gather | bytes 557056 | tf_op jit(solution)/shard_map/all_gather | solution.py:175
  293.8 0.1 multiply_multiply_fusion
  293.9 0.1 reshape.197
  294.1 0.1 reshape.198
  294.2 1.9 fusion.22
  296.1 1.9 fusion.27
  298.1 0.1 add_reduce_fusion
  298.2 0.3 fusion.80
  298.5 0.3 fusion.77
  298.8 0.3 fusion.5
  299.2 0.3 fusion.3
  299.5 97.3 %all-reduce = (f32[32,128]{1,0:T(8,128)S(1)}, f32[32,128]{1,0:T(8,128)S(1)}) all-reduce(f32[32,128]{1,0:T(8,128)S(1)} %fusion.3, f32[32,128]{1,0:T(8,128)S(1)} %fusion.5), channel_id=1, replica_groups=mesh['src'=16,'rows'=32] {'src','rows'}, use_global_device_ids=true, to_apply=%region_9.10 | all-reduce | flops 8192 | bytes 65536 | tf_op jit(solution)/shard_map/psum | solution.py:185
  396.9 0.3 fusion.35
  397.1 0.3 fusion.31
  397.4 0.3 convolution_subtract_fusion.3
  397.6 0.3 multiply_add_fusion.1
  397.9 1.3 fusion.20
  399.2 1.9 fusion.1
  (7 shorter events, 0.1 us)
Async XLA Ops:
  6.5 256.0 %reduce-scatter.2.cloned.1.call-start = ((), (), s32[]{:S(2)}) async-start(), calls=%async_computation.1 | async-start | bytes 557056 | tf_op jit(solution)/shard_map/reduce_scatter | solution.py:173
  12.8 0.7 copy-start.1
  14.0 0.7 copy-start.2
  150.2 0.7 copy-start.3
  154.2 108.4 %copy-start = (s32[16,512]{1,0:T(8,128)S(1)}, s32[16,512]{1,0:T(8,128)}, u32[]{:S(2)}) copy-start(s32[16,512]{1,0:T(8,128)} %param.6) | copy-start | bytes 98308
Sparse Core Ops, SparseCore 0:
  154.3 108.1 reduce-scatter.1
where the time goes:
time: 408 us
  blocking collectives  257 us (63%)
  waiting for transfers between devices  108 us (26%)
  matrix products  18.8 us (5%)
  between operations  14.3 us (4%)
  other arithmetic  6.64 us (2%)
    psum x1, blocking collectives, local(): lax.psum((part_real * unit_scale, part_imag * unit_scale), 'rows')  129 us
    reduce_scatter x1, waiting for transfers between devices, local(): lax.psum_scatter(intensity_part, 'src', scatter_dimension=1, tiled=True)  108 us
    psum x1, blocking collectives, local(): lax.psum((adjoint_real * unit_scale, adjoint_imag * unit_scale), ('src',...  97.3 us
    all_gather x1, blocking collectives, local(): slope = lax.all_gather(slope_share, 'src', axis=1, tiled=True)  30.5 us
    dot_general x12, matrix products, product(): jnp.dot(matrix_left, matrix_right, precision=highest, preferred_element_t...  8.99 us
  transfers between devices with their start and end apart: 1, of which 1 were waited for; matrix products, arithmetic and copies ran while one was open for 0% of the time, Pallas kernels for 0%

commit v1 on v0

--- a/solution.py
+++ b/solution.py
@@ -8,6 +8,11 @@
 threshold_level = 0.25
 loss_weight = 8.0
 highest = lax.Precision.HIGHEST
+
+
+def axis_by_axis(value, axis_one, axis_two):
+    inner = lax.psum(value, axis_one)
+    return lax.psum(inner, axis_two)
 
 
 def product(matrix_left, matrix_right):
@@ -182,8 +187,8 @@
     back_real, back_imag = rows_forward(cot_real, cot_imag, row_start, band_rows, total_rows)
     adjoint_real = pupil_list[source_point] * back_real
     adjoint_imag = pupil_list[source_point] * back_imag
-    adjoint_real, adjoint_imag = lax.psum(
-        (adjoint_real * unit_scale, adjoint_imag * unit_scale), ("src", "rows")
+    adjoint_real, adjoint_imag = axis_by_axis(
+        (adjoint_real * unit_scale, adjoint_imag * unit_scale), "rows", "src"
     )
     head_real, head_imag = rows_inverse(
         adjoint_real * unit_scale, adjoint_imag * unit_scale, row_start, row_block, total_rows

time: 408 us -> 542 us (1.33)
  blocking collectives: 257 us -> 387 us
    psum x1 -> x2, blocking collectives: 97.3 us -> 228 us  [the longest x1 124 us: axis_by_axis(): inner = lax.psum(value, axis_one)]
where the time goes in v1:
time: 542 us; the launch traced here: 539 us
  blocking collectives  387 us (71%)
  waiting for transfers between devices  108 us (20%)
  matrix products  18.8 us (3%)
  between operations  14.3 us (3%)
  other arithmetic  6.64 us (1%)
    psum x1, blocking collectives, local(): lax.psum((part_real * unit_scale, part_imag * unit_scale), 'rows')  129 us
    psum x1, blocking collectives, axis_by_axis(): inner = lax.psum(value, axis_one)  124 us
    reduce_scatter x1, waiting for transfers between devices, local(): lax.psum_scatter(intensity_part, 'src', scatter_dimension=1, tiled=True)  108 us
    psum x1, blocking collectives, axis_by_axis(): return lax.psum(inner, axis_two)  104 us
    all_gather x1, blocking collectives, local(): slope = lax.all_gather(slope_share, 'src', axis=1, tiled=True)  30.5 us
  transfers between devices with their start and end apart: 1, of which 1 were waited for; matrix products, arithmetic and copies ran while one was open for 0% of the time, Pallas kernels for 0%

profile of v1, /device:TPU:1, one launch (start us, length us, event | category | flops | bytes accessed | tf_op | source)
XLA Modules:
  0.0 538.7 jit_solution(10749562180551666673)
XLA Ops:
  6.5 0.0 reduce-scatter.2.cloned.1.call-start
  6.5 1.2 add_divide_fusion
  7.7 0.1 reshape.193
  7.8 0.1 fusion.73
  8.0 1.5 convolution_negate_fusion
  9.5 0.3 copy.6
  9.9 1.6 add_reduce_fusion.1
  11.4 0.3 fusion.86
  11.8 0.3 fusion.83
  12.1 0.3 fusion.7
  12.4 0.3 fusion.6
  12.8 0.0 copy-start.1
  12.8 0.6 copy-done.1
  13.5 0.6 dynamic_slice.13
  14.0 0.0 copy-start.2
  14.0 0.7 multiply_multiply_fusion.2
  14.7 0.0 copy-done.2
  14.7 0.6 dynamic_slice.12
  15.3 0.7 multiply_multiply_fusion.3
  16.0 128.9 %all-reduce.1 = (f32[32,128]{1,0:T(8,128)S(1)}, f32[32,128]{1,0:T(8,128)S(1)}) all-reduce(f32[32,128]{1,0:T(8,128)S(1)} %fusion.6, f32[32,128]{1,0:T(8,128)S(1)} %fusion.7), channel_id=1, replica_groups=mesh['src'=16,'rows'=32] {'rows'}, use_global_device_ids=true, to_apply=%region_4.5 | all-reduce | flops 8192 | bytes 65536 | tf_op jit(solution)/shard_map/psum | solution.py:161
  144.9 0.2 fusion.37
  145.1 0.3 fusion.38
  145.4 0.3 convolution_subtract_fusion.4
  145.6 0.3 convolution_add_fusion.3
  145.9 1.9 fusion.16
  147.9 1.9 fusion.17
  149.8 0.2 slice_add_fusion
  150.0 0.1 reshape.195
  150.2 0.0 copy-start.3
  150.2 0.1 reshape.196
  150.3 0.5 copy-done.3
  150.8 0.6 reduce_sum.45
  151.4 0.6 broadcast_divide_fusion
  152.1 0.6 dynamic_slice.14
  152.7 1.5 add_multiply_fusion
  154.2 0.0 copy-start
  154.2 0.0 reduce-scatter.2.cloned.1.call-update
  154.8 0.1 fusion.123
  154.9 107.6 %reduce-scatter.2.cloned.1.call-done = f32[16,512]{1,0:T(8,128)} async-done(((f32[16,8192]{1,0:T(8,128)}), f32[16,512]{1,0:T(8,128)}) %reduce-scatter.2.cloned.1.call-update) | async-done | bytes 32784 | tf_op jit(solution)/shard_map/reduce_scatter | solution.py:178
  262.5 0.0 copy-done
  262.5 0.8 subtract_multiply_fusion
  263.3 30.5 %all_gather.3 = f32[16,8192]{1,0:T(8,128)S(1)} all-gather(f32[16,512]{1,0:T(8,128)S(1)} %subtract_multiply_fusion), channel_id=1, replica_groups=mesh['src'=16,'rows'=32] {'src'}, dimensions={1}, use_global_device_ids=true | all-gather | bytes 557056 | tf_op jit(solution)/shard_map/all_gather | solution.py:180
  293.8 0.1 multiply_multiply_fusion
  293.9 0.1 reshape.197
  294.1 0.1 reshape.198
  294.2 1.9 fusion.22
  296.1 1.9 fusion.27
  298.1 0.1 add_reduce_fusion
  298.2 0.3 fusion.80
  298.5 0.3 fusion.77
  298.8 0.3 fusion.5
  299.2 0.3 fusion.3
  299.5 124.2 %all-reduce = (f32[32,128]{1,0:T(8,128)S(1)}, f32[32,128]{1,0:T(8,128)S(1)}) all-reduce(f32[32,128]{1,0:T(8,128)S(1)} %fusion.3, f32[32,128]{1,0:T(8,128)S(1)} %fusion.5), channel_id=1, replica_groups=mesh['src'=16,'rows'=32] {'rows'}, use_global_device_ids=true, to_apply=%region_10.11 | all-reduce | flops 8192 | bytes 65536 | tf_op jit(solution)/shard_map/psum | solution.py:14
  423.7 103.9 %all-reduce.2 = (f32[32,128]{1,0:T(8,128)S(1)}, f32[32,128]{1,0:T(8,128)S(1)}) all-reduce(f32[32,128]{1,0:T(8,128)S(1)} %get-tuple-element.9, f32[32,128]{1,0:T(8,128)S(1)} %get-tuple-element.10), channel_id=1, replica_groups=mesh['src'=16,'rows'=32] {'src'}, use_global_device_ids=true, to_apply=%region_11.12 | all-reduce | flops 8192 | bytes 65536 | tf_op jit(solution)/shard_map/psum | solution.py:15
  527.6 0.3 fusion.35
  527.9 0.3 fusion.31
  528.1 0.3 convolution_subtract_fusion.3
  528.4 0.3 multiply_add_fusion.1
  528.6 1.3 fusion.20
  529.9 1.9 fusion.1
  (7 shorter events, 0.1 us)
Async XLA Ops:
  6.5 256.0 %reduce-scatter.2.cloned.1.call-start = ((), (), s32[]{:S(2)}) async-start(), calls=%async_computation.1 | async-start | bytes 557056 | tf_op jit(solution)/shard_map/reduce_scatter | solution.py:178
  12.8 0.7 copy-start.1
  14.0 0.7 copy-start.2
  150.2 0.7 copy-start.3
  154.2 108.4 %copy-start = (s32[16,512]{1,0:T(8,128)S(1)}, s32[16,512]{1,0:T(8,128)}, u32[]{:S(2)}) copy-start(s32[16,512]{1,0:T(8,128)} %param.6) | copy-start | bytes 98308
Sparse Core Ops, SparseCore 0:
  154.3 108.1 reduce-scatter.1
